TPU v7x, 32 devices: a whole 2x2x4 slice. The times are simulated.
32 devices in a mesh: tm: 8 (over z, x), space: 4 (over y, core).
Axes of the slice: x: 2, y: 2, z: 4, core: 2. Of those that a mesh axis runs over, the one named last changes fastest.
Arguments:
- queries: bfloat16 [8, 512, 2048], P('tm', 'space'), may hold values from -180 to 180
- key_vectors: bfloat16 [8, 512, 2048], P('tm', 'space'), may hold values from -6 to 6
- value_vectors: bfloat16 [8, 512, 2048], P('tm', 'space'), may hold values from -96 to 96
- block_lists: int32 [4, 3], replicated, may hold values from 0 to 3, as said below
- step_sizes: float32 [8, 512, 16], P(None, ('space', 'tm')), may hold values from 0.004 to 0.6, as said below
- decay_rates: float32 [16], replicated, may hold values from 0.7 to 1.4
- skip_gains: float32 [16], replicated, may hold values from 0.5 to 1.5
- pre_gain: float32 [2048], replicated, may hold values from 0.25 to 1.75
- state_in_weight: bfloat16 [2048, 64], replicated, may hold values from -0.125 to 0.125
- state_out_weight: bfloat16 [2048, 64], replicated, may hold values from -0.125 to 0.125
- post_gain: float32 [2048], replicated, may hold values from 0.25 to 1.75
Outputs:
- mixed_out: bfloat16 [8, 512, 2048], P('tm', 'space')
Inputs may be any that keep to these rules, and one draw needn't show every extreme that they name: `block_lists`: row i lists 3 different key blocks; its first entry is i itself. `step_sizes`: positive step sizes.
All inputs are finite; a program needn't handle non-finite values.
Results may differ from a plain program's by a relative error of at most 0.01.
Values may be sent and summed in bfloat16 or wider, within the bound.
A program may use at most 64 MiB of HBM per device.

v0:
```python
import math

import jax
import jax.numpy as jnp
from jax import lax
from jax.sharding import PartitionSpec as P

SHARED_HEADS = 16
HEAD_DIM = 128
BLOCK = 128


def rms_scale(values, gain_row):
    return values * lax.rsqrt(jnp.mean(values * values, axis=-1, keepdims=True) + 1e-05) * gain_row


def attend_heads(stacked, block_lists):
    query_rows, key_rows, value_rows = stacked
    total_rows, head_count, head_width = query_rows.shape
    block_count = total_rows // BLOCK
    group_size = math.gcd(block_count, max(1, 512 // BLOCK))
    list_width = block_lists.shape[1]
    score_scale = 1.0 / math.sqrt(head_width)
    query_blocks = query_rows.reshape(block_count, BLOCK, head_count, head_width)
    key_blocks = key_rows.reshape(block_count, BLOCK, head_count, head_width)
    value_blocks = value_rows.reshape(block_count, BLOCK, head_count, head_width)

    def attend_group(group_index):
        first_block = group_index * group_size
        chosen = lax.dynamic_slice_in_dim(block_lists, first_block, group_size, 0)
        query_group = lax.dynamic_slice_in_dim(query_blocks, first_block, group_size, 0)
        key_group = jnp.take(key_blocks, chosen, axis=0).reshape(
            group_size, list_width * BLOCK, head_count, head_width
        )
        value_group = jnp.take(value_blocks, chosen, axis=0).reshape(
            group_size, list_width * BLOCK, head_count, head_width
        )
        scores = (
            jnp.einsum(
                "gqhd,gkhd->ghqk", query_group, key_group, preferred_element_type=jnp.float32
            )
            * score_scale
        )
        row_max = jnp.max(scores, axis=-1, keepdims=True)
        exp_scores = jnp.exp(scores - row_max)
        totals = jnp.sum(exp_scores, axis=-1)
        weights_bf = exp_scores.astype(jnp.bfloat16)
        summed = jnp.einsum(
            "ghqk,gkhd->gqhd", weights_bf, value_group, preferred_element_type=jnp.float32
        )
        return (summed / jnp.transpose(totals, (0, 2, 1))[..., None]).astype(jnp.bfloat16)

    attended = lax.map(attend_group, jnp.arange(block_count // group_size, dtype=jnp.int32))
    return attended.reshape(total_rows, head_count, head_width)


def attend_grouped(stacked, block_lists):
    query_rows, key_rows, value_rows = stacked
    total_rows = query_rows.shape[0]
    head_count = query_rows.shape[2]
    head_width = query_rows.shape[3]
    flat = tuple(
        (
            piece.reshape(total_rows, head_count, head_width)
            for piece in (query_rows, key_rows, value_rows)
        )
    )
    result = attend_heads(flat, block_lists)
    return result.reshape(total_rows, 1, head_count, head_width)


def temporal_mix(
    normed, step_block, decay_rates, skip_gains, state_in_weight, state_out_weight, post_gain
):
    frame_count, token_count, channel_count = normed.shape
    head_count = step_block.shape[2]
    head_width = channel_count // head_count
    flat_rows = normed.reshape(frame_count * token_count, channel_count)
    b_in = jnp.dot(flat_rows, state_in_weight, preferred_element_type=jnp.float32).reshape(
        frame_count, token_count, -1
    )
    c_out = jnp.dot(flat_rows, state_out_weight, preferred_element_type=jnp.float32).reshape(
        frame_count, token_count, -1
    )
    gram_matrix = jnp.einsum("tkn,skn->kts", c_out, b_in, precision=lax.Precision.HIGHEST)
    log_decay = -step_block * decay_rates
    frame_index = jnp.arange(frame_count, dtype=jnp.int32)
    between = (
        (frame_index[None, :, None] < frame_index[None, None, :])
        & (frame_index[None, None, :] <= frame_index[:, None, None])
    ).astype(jnp.float32)
    seg_sum = jnp.einsum("tsr,rkh->ktsh", between, log_decay, precision=lax.Precision.HIGHEST)
    causal = frame_index[None, :] <= frame_index[:, None]
    decay_matrix = jnp.where(causal[None, :, :, None], jnp.exp(seg_sum), jnp.zeros_like(seg_sum))
    weight_matrix = (
        gram_matrix[..., None] * decay_matrix * jnp.transpose(step_block, (1, 0, 2))[:, None, :, :]
    )
    x_values = normed.astype(jnp.float32).reshape(frame_count, token_count, head_count, head_width)
    y_mixed = (
        jnp.einsum("ktsh,skhp->tkhp", weight_matrix, x_values, precision=lax.Precision.HIGHEST)
        + skip_gains[:, None] * x_values
    )
    y_flat = y_mixed.reshape(frame_count, token_count, channel_count)
    return rms_scale(y_flat, post_gain).astype(jnp.bfloat16)


def body(
    queries,
    key_vectors,
    value_vectors,
    block_lists,
    step_sizes,
    decay_rates,
    skip_gains,
    pre_gain,
    state_in_weight,
    state_out_weight,
    post_gain,
):
    token_count = queries.shape[1]
    channel_count = queries.shape[2]
    query_rows = queries.reshape(token_count, SHARED_HEADS, HEAD_DIM)
    key_rows = key_vectors.reshape(token_count, SHARED_HEADS, HEAD_DIM)
    value_rows = value_vectors.reshape(token_count, SHARED_HEADS, HEAD_DIM)
    by_token = None
    attended = None
    space_count = lax.axis_size("space")
    local_heads = SHARED_HEADS // space_count
    query_split = query_rows.reshape(token_count, space_count, local_heads, HEAD_DIM)
    key_split = key_rows.reshape(token_count, space_count, local_heads, HEAD_DIM)
    value_split = value_rows.reshape(token_count, space_count, local_heads, HEAD_DIM)
    received = attend_grouped(
        (
            lax.all_to_all(query_split, "space", split_axis=1, concat_axis=0, tiled=True),
            lax.all_to_all(key_split, "space", split_axis=1, concat_axis=0, tiled=True),
            lax.all_to_all(value_split, "space", split_axis=1, concat_axis=0, tiled=True),
        ),
        block_lists=block_lists,
    )
    gathered = received.reshape(received.shape[0], local_heads, HEAD_DIM)
    attended = lax.all_to_all(gathered, "space", split_axis=0, concat_axis=1, tiled=True)
    normed = rms_scale(
        attended.reshape(1, token_count, channel_count).astype(jnp.float32), pre_gain
    ).astype(jnp.bfloat16)
    by_token = lax.all_to_all(normed, "tm", split_axis=1, concat_axis=0, tiled=True)
    mixed_tokens = temporal_mix(
        by_token, step_sizes, decay_rates, skip_gains, state_in_weight, state_out_weight, post_gain
    )
    return lax.all_to_all(mixed_tokens, "tm", split_axis=0, concat_axis=1, tiled=True)


def solution(mesh):
    placed = (
        P("tm", "space", None),
        P("tm", "space", None),
        P("tm", "space", None),
        P(),
        P(None, ("space", "tm"), None),
        P(),
        P(),
        P(),
        P(),
        P(),
        P(),
    )
    return jax.shard_map(
        body, mesh=mesh, in_specs=placed, out_specs=P("tm", "space", None), check_vma=False
    )
```

profile of v0, /device:TPU:0, one launch (start us, length us, event | category | flops | bytes accessed | tf_op | source)
XLA Modules:
  0.0 110.1 jit_solution(432417027500597041)
XLA Ops:
  0.0 1.4 %copy.111 = bf16[1,128,2048]{1,2,0:T(8,128)(2,1)S(1)} copy(bf16[1,128,2048]{2,1,0:T(8,128)(2,1)} %param.14) | data formatting | bytes 1048576 | tf_op args[1]
  1.4 1.1 copy.112
  2.5 4.2 %all-to-all-start.1 = ((bf16[128,4,4,128]{3,2,0,1:T(4,128)(2,1)}), bf16[128,4,4,128]{3,2,0,1:T(4,128)(2,1)S(1)}, u32[]{:S(2)}, u32[]{:S(2)}) async-start(bf16[128,4,4,128]{3,2,0,1:T(4,128)(2,1)} %copy.112), calls=%async_computation.1 | async-start | bytes 1048576 | tf_op jit(solution)/shard_map/all_to_all | solution.py:135
  6.7 0.3 copy.108
  7.0 1.1 copy.109
  8.1 7.5 %all-to-all-done.1 = bf16[128,4,4,128]{3,2,0,1:T(4,128)(2,1)S(1)} async-done(((bf16[128,4,4,128]{3,2,0,1:T(4,128)(2,1)}), bf16[128,4,4,128]{3,2,0,1:T(4,128)(2,1)S(1)}, u32[]{:S(2)}, u32[]{:S(2)}) %all-to-all-start.1) | async-done | bytes 524320 | tf_op jit(solution)/shard_map/all_to_all | solution.py:135
  15.5 3.5 %all-to-all-start = ((bf16[128,4,4,128]{3,2,0,1:T(4,128)(2,1)}), bf16[128,4,4,128]{3,2,0,1:T(4,128)(2,1)S(1)}, u32[]{:S(2)}, u32[]{:S(2)}) async-start(bf16[128,4,4,128]{3,2,0,1:T(4,128)(2,1)} %copy.109), calls=%async_computation | async-start | bytes 1048576 | tf_op jit(solution)/shard_map/all_to_all | solution.py:136
  19.1 0.3 copy.114
  19.4 1.0 copy.115
  20.4 1.9 %gather_fusion.1 = bf16[12,128,4,128]{3,2,1,0:T(4,128)(2,1)S(1)} fusion(bf16[4,128,4,128]{3,2,1,0:T(4,128)(2,1)S(1)} %bitcast.92, s32[1024]{0:T(1024)S(1)} %pad_clamp_fusion), kind=kCustom, calls=%fused_computation.1.clone | custom fusion | bytes 3145776 | tf_op jit(solution)/shard_map/while/body/eval_jaxpr/jit(_take)/gather | solution.py:32
  22.4 5.5 %all-to-all-done = bf16[128,4,4,128]{3,2,0,1:T(4,128)(2,1)S(1)} async-done(((bf16[128,4,4,128]{3,2,0,1:T(4,128)(2,1)}), bf16[128,4,4,128]{3,2,0,1:T(4,128)(2,1)S(1)}, u32[]{:S(2)}, u32[]{:S(2)}) %all-to-all-start) | async-done | bytes 524320 | tf_op jit(solution)/shard_map/all_to_all | solution.py:136
  27.8 3.5 %all-to-all-start.2 = ((bf16[128,4,4,128]{3,0,2,1:T(8,128)(2,1)}), bf16[128,4,4,128]{3,0,2,1:T(8,128)(2,1)S(1)}, u32[]{:S(2)}, u32[]{:S(2)}) async-start(bf16[128,4,4,128]{3,0,2,1:T(8,128)(2,1)} %copy.115), calls=%async_computation.2 | async-start | bytes 1048576 | tf_op jit(solution)/shard_map/all_to_all | solution.py:134
  31.3 3.2 %gather_fusion = bf16[12,128,4,128]{3,2,1,0:T(4,128)(2,1)} fusion(bf16[4,128,4,128]{3,2,1,0:T(4,128)(2,1)S(1)} %bitcast.93, s32[1024]{0:T(1024)S(1)} %pad_clamp_fusion), kind=kCustom, calls=%fused_computation.clone | custom fusion | bytes 3145776 | tf_op jit(solution)/shard_map/while/body/eval_jaxpr/jit(_take)/gather | solution.py:35
  34.5 2.8 %broadcast_select_fusion = (bf16[4,3,128,4,128]{4,3,2,1,0:T(4,128)(2,1)S(1)}, bf16[4,3,128,4,128]{4,3,2,1,0:T(4,128)(2,1)S(1)}) fusion(bf16[4,3,128,4,128]{4,3,2,1,0:T(4,128)(2,1)S(1)} %bitcast.95, pred[4,3]{1,0:T(4,128)(4,1)S(1)} %compare_and_fusion, bf16[4,3,128,4,128]{4,3,2,1,0:T(4,128)(2,1)} %bitcast.96), kind=kLoop, calls=%fused_computation.10 | loop fusion | flops 1572864 | bytes 6291468 | tf_op jit(solution)/shard_map/while/body/eval_jaxpr/jit(_take)/select_n | solution.py:32
  37.3 1.6 %copy.110 = bf16[4,3,128,4,128]{4,2,1,3,0:T(8,128)(2,1)} copy(bf16[4,3,128,4,128]{4,3,2,1,0:T(4,128)(2,1)S(1)} %get-tuple-element.17) | data formatting | bytes 3145728 | tf_op jit(solution)/shard_map/while/body/eval_jaxpr/jit(_take)/select_n | solution.py:35
  38.9 0.4 copy.113
  39.3 0.9 all-to-all-done.2
  40.1 0.6 bitcast_reduce_fusion
  40.7 0.5 fusion.1
  41.3 0.9 copy-done.1
  42.1 1.0 fusion.18
  43.2 0.4 copy.118
  43.6 11.2 %all_to_all.75 = bf16[512,4,128]{2,1,0:T(4,128)(2,1)S(1)} all-to-all(bf16[512,4,128]{2,1,0:T(4,128)(2,1)S(1)} %copy.118), channel_id=1, replica_groups=mesh['tm'=8,'space'=4] {'space'}, dimensions={0} | all-to-all | bytes 1048576 | tf_op jit(solution)/shard_map/all_to_all | solution.py:141
  54.9 0.3 copy.120
  55.2 0.2 multiply_reduce_fusion.1
  55.6 0.3 multiply_convert_fusion.1
  55.9 0.9 copy.121
  56.9 0.5 broadcast.154
  57.4 3.7 %reduce.7 = bf16[128,2048]{1,0:T(8,128)(2,1)S(1)} reduce(bf16[128,1,2048]{2,1,0:T(2,128)(2,1)S(1)} %bitcast.100, bf16[]{:T(256)} %broadcast.154), dimensions={1}, to_apply=%bitcast.81.reduce_sub_computation | reduce | bytes 1048578
  61.2 1.2 %reshape.227 = bf16[8,2,16384]{2,1,0:T(2,128)(2,1)} reshape(bf16[128,2048]{1,0:T(8,128)(2,1)S(1)} %reduce.7) | data formatting | bytes 1048576
  62.3 6.5 %all-to-all-start.4 = ((bf16[8,2,16384]{2,1,0:T(2,128)(2,1)}), bf16[8,2,16384]{2,1,0:T(2,128)(2,1)S(1)}, u32[]{:S(2)}, u32[]{:S(2)}) async-start(bf16[8,2,16384]{2,1,0:T(2,128)(2,1)} %reshape.227), calls=%async_computation.4 | async-start | bytes 1048576 | tf_op jit(solution)/shard_map/all_to_all | solution.py:145
  68.9 14.1 %all-to-all-done.4 = bf16[8,2,16384]{2,1,0:T(2,128)(2,1)S(1)} async-done(((bf16[8,2,16384]{2,1,0:T(2,128)(2,1)}), bf16[8,2,16384]{2,1,0:T(2,128)(2,1)S(1)}, u32[]{:S(2)}, u32[]{:S(2)}) %all-to-all-start.4) | async-done | bytes 524320 | tf_op jit(solution)/shard_map/all_to_all | solution.py:145
  82.9 0.5 reshape.228
  83.5 3.0 %bitcast_reduce_fusion.2 = bf16[128,2048]{1,0:T(8,128)(2,1)S(1)} fusion(bf16[128,1,2048]{2,1,0:T(2,128)(2,1)S(1)} %reshape.228), kind=kLoop, calls=%fused_computation.52 | loop fusion | bytes 1048576 | tf_op jit(solution)/shard_map/all_to_all | solution.py:145
  86.6 0.3 copy.135
  86.9 0.3 fusion.24
  87.2 0.2 copy-done.4
  87.4 0.3 fusion.26
  87.7 0.3 fusion.29
  88.0 0.4 fusion.14
  88.4 0.4 copy.127
  88.9 1.4 %multiply_reduce_fusion = (f32[8,16]{0,1:T(8,128)S(1)}, f32[8,16,16,128]{3,0,2,1:T(8,128)S(1)}) fusion(bf16[8,16,16,128]{3,2,1,0:T(8,128)(2,1)S(1)} %bitcast.108, f32[16]{0:T(128)S(1)} %copy-done.10, f32[16,8,8,16]{2,1,3,0:T(8,128)S(1)} %copy.127), kind=kOutput, calls=%fused_computation.23 | convolution fusion | flops 26476416 | bytes 1638976 | tf_op jit(solution)/shard_map/ktsh,skhp->tkhp/dot_general | solution.py:100
  90.3 0.2 copy.129
  90.5 0.2 reshape.191
  90.8 0.4 copy-done.7
  91.2 0.2 multiply_convert_fusion
  91.4 17.9 %all_to_all.76 = bf16[8,16,2048]{2,1,0:T(8,128)(2,1)S(1)} all-to-all(bf16[8,16,2048]{2,1,0:T(8,128)(2,1)S(1)} %multiply_convert_fusion), channel_id=1, replica_groups=mesh['tm'=8,'space'=4] {'tm'}, dimensions={0} | all-to-all | bytes 1048576 | tf_op jit(solution)/shard_map/all_to_all | solution.py:149
  109.3 0.8 copy.151
  (33 shorter events, 0.6 us)
Async XLA Ops:
  0.0 86.9 %copy-start = (bf16[2048,64]{0,1:T(8,128)(2,1)S(1)}, bf16[2048,64]{0,1:T(8,128)(2,1)}, u32[]{:S(2)}) copy-start(bf16[2048,64]{0,1:T(8,128)(2,1)} %param.21) | copy-start | bytes 786436
  0.0 6.7 %copy-start.2 = (bf16[1,128,2048]{2,1,0:T(8,128)(2,1)S(1)}, bf16[1,128,2048]{2,1,0:T(8,128)(2,1)}, u32[]{:S(2)}) copy-start(bf16[1,128,2048]{2,1,0:T(8,128)(2,1)} %param.15) | copy-start | bytes 1572868
  2.5 13.1 %all-to-all-start.1 = ((bf16[128,4,4,128]{3,2,0,1:T(4,128)(2,1)}), bf16[128,4,4,128]{3,2,0,1:T(4,128)(2,1)S(1)}, u32[]{:S(2)}, u32[]{:S(2)}) async-start(bf16[128,4,4,128]{3,2,0,1:T(4,128)(2,1)} %copy.112), calls=%async_computation.1 | async-start | bytes 1048576 | tf_op jit(solution)/shard_map/all_to_all | solution.py:135
  6.7 12.3 %copy-start.8 = (s32[4,3]{1,0:T(4,128)S(1)}, s32[4,3]{1,0:T(4,128)}, u32[]{:S(2)}) copy-start(s32[4,3]{1,0:T(4,128)} %param.16) | copy-start | bytes 148
  6.7 12.4 %copy-start.3 = (bf16[1,128,2048]{2,1,0:T(8,128)(2,1)S(1)}, bf16[1,128,2048]{2,1,0:T(8,128)(2,1)}, u32[]{:S(2)}) copy-start(bf16[1,128,2048]{2,1,0:T(8,128)(2,1)} %param.13) | copy-start | bytes 1572868
  15.5 12.3 %all-to-all-start = ((bf16[128,4,4,128]{3,2,0,1:T(4,128)(2,1)}), bf16[128,4,4,128]{3,2,0,1:T(4,128)(2,1)S(1)}, u32[]{:S(2)}, u32[]{:S(2)}) async-start(bf16[128,4,4,128]{3,2,0,1:T(4,128)(2,1)} %copy.109), calls=%async_computation | async-start | bytes 1048576 | tf_op jit(solution)/shard_map/all_to_all | solution.py:136
  27.8 12.3 %all-to-all-start.2 = ((bf16[128,4,4,128]{3,0,2,1:T(8,128)(2,1)}), bf16[128,4,4,128]{3,0,2,1:T(8,128)(2,1)S(1)}, u32[]{:S(2)}, u32[]{:S(2)}) async-start(bf16[128,4,4,128]{3,0,2,1:T(8,128)(2,1)} %copy.115), calls=%async_computation.2 | async-start | bytes 1048576 | tf_op jit(solution)/shard_map/all_to_all | solution.py:134
  40.7 1.4 %copy-start.1 = (bf16[4,3,128,4,128]{4,2,1,3,0:T(8,128)(2,1)S(1)}, bf16[4,3,128,4,128]{4,2,1,3,0:T(8,128)(2,1)}, u32[]{:S(2)}) copy-start(bf16[4,3,128,4,128]{4,2,1,3,0:T(8,128)(2,1)} %copy.110) | copy-start | bytes 4718596
  54.9 0.7 copy-start.6
  57.4 11.4 %copy-start.5 = (f32[8,16,16]{2,1,0:T(8,128)S(1)}, f32[8,16,16]{2,1,0:T(8,128)}, u32[]{:S(2)}) copy-start(f32[8,16,16]{2,1,0:T(8,128)} %param.17) | copy-start | bytes 24580
  57.4 11.4 %copy-start.9 = (f32[16]{0:T(128)S(1)}, f32[16]{0:T(128)}, u32[]{:S(2)}) copy-start(f32[16]{0:T(128)} %param.18) | copy-start | bytes 196
  62.3 20.6 %all-to-all-start.4 = ((bf16[8,2,16384]{2,1,0:T(2,128)(2,1)}), bf16[8,2,16384]{2,1,0:T(2,128)(2,1)S(1)}, u32[]{:S(2)}, u32[]{:S(2)}) async-start(bf16[8,2,16384]{2,1,0:T(2,128)(2,1)} %reshape.227), calls=%async_computation.4 | async-start | bytes 1048576 | tf_op jit(solution)/shard_map/all_to_all | solution.py:145
  86.5 1.0 copy-start.4
  87.7 1.1 %copy-start.10 = (f32[16]{0:T(128)S(1)}, f32[16]{0:T(128)}, u32[]{:S(2)}) copy-start(f32[16]{0:T(128)} %param.19) | copy-start | bytes 196
  90.5 0.7 copy-start.7
where the time goes:
time: 111 us; the launch traced here: 110 us
  blocking collectives  29.1 us (26%)
  waiting for transfers between devices  27.9 us (25%)
  local copies, waits for them, and re-layouts  22.8 us (21%)
  starting transfers between devices  17.6 us (16%)
  other arithmetic  7.92 us (7%)
  matrix products  4.28 us (4%)
    all_to_all x1, blocking collectives, body(): lax.all_to_all(mixed_tokens, 'tm', split_axis=0, concat_axis=1, tiled=True)  17.9 us
    all_to_all x1, waiting for transfers between devices, body(): lax.all_to_all(normed, 'tm', split_axis=1, concat_axis=0, tiled=True)  14.1 us
    all_to_all x1, blocking collectives, body(): lax.all_to_all(gathered, 'space', split_axis=0, concat_axis=1, tiled=True)  11.2 us
    all_to_all x1, waiting for transfers between devices, body(): lax.all_to_all(key_split, 'space', split_axis=1, concat_axis=0, tiled=True)  7.49 us
    unnamed x31, local copies, waits for them, and re-layouts  7.03 us
    all_to_all x1, starting transfers between devices, body(): lax.all_to_all(normed, 'tm', split_axis=1, concat_axis=0, tiled=True)  6.46 us
    all_to_all x1, waiting for transfers between devices, body(): lax.all_to_all(value_split, 'space', split_axis=1, concat_axis=0, tiled=T...  5.49 us
    all_to_all x1, starting transfers between devices, body(): lax.all_to_all(key_split, 'space', split_axis=1, concat_axis=0, tiled=True)  4.24 us
  transfers between devices with their start and end apart: 4, of which 4 were waited for; matrix products, arithmetic and copies ran while one was open for 11% of the time, Pallas kernels for 0%

commit v1 on v0

v1 whole, which is shorter than its diff:
```python
import functools
import math

import jax
import jax.numpy as jnp
from jax import lax
from jax.experimental import pallas as pl
from jax.experimental.pallas import tpu as pltpu
from jax.sharding import PartitionSpec as P

SHARED_HEADS = 16
HEAD_DIM = 128
BLOCK = 128
GROUPS = 4
MESH = pl.DeviceIdType.MESH
F32 = jnp.float32
BF16 = jnp.bfloat16


def remote(src, dst, send_sem, recv_sem, axis, index):
    return pltpu.make_async_remote_copy(
        src_ref=src,
        dst_ref=dst,
        send_sem=send_sem,
        recv_sem=recv_sem,
        device_id={axis: index},
        device_id_type=MESH,
    )


def kernel(
    dims,
    lists_ref,
    rates_ref,
    skips_ref,
    q_ref,
    k_ref,
    v_ref,
    steps_ref,
    pre_ref,
    w_in_ref,
    w_out_ref,
    post_ref,
    out_ref,
    kv_buf,
    a_buf,
    x_buf,
    n_buf,
    y_buf,
    o_buf,
    d_buf,
    own_sem,
    kv_send,
    kv_recv,
    relay_send,
    relay_recv,
    a_send,
    a_recv,
    o_send,
    o_recv,
    self_sem,
):
    space_count, tm_count, list_width = dims
    tokens, channels = q_ref.shape
    rows = tokens // tm_count
    width = channels // GROUPS
    heads_here = width // HEAD_DIM
    chips = space_count // 2
    space = lax.axis_index("space")
    tm = lax.axis_index("tm")
    chip = space // 2
    core = space % 2
    partner = chip * 2 + 1 - core

    barrier = pltpu.get_barrier_semaphore()

    def greet_chip(step, carry):
        peer = lax.rem(chip + step, chips) * 2 + core
        pl.semaphore_signal(barrier, inc=1, device_id={"space": peer}, device_id_type=MESH)
        return carry

    def greet_frame(step, carry):
        peer = lax.rem(tm + step, tm_count)
        pl.semaphore_signal(barrier, inc=1, device_id={"tm": peer}, device_id_type=MESH)
        return carry

    pl.semaphore_signal(barrier, inc=1, device_id={"space": partner}, device_id_type=MESH)
    lax.fori_loop(1, chips, greet_chip, 0)
    lax.fori_loop(1, tm_count, greet_frame, 0)

    def own_copy(which, group):
        source = (k_ref, v_ref)[which]
        return pltpu.make_async_copy(
            source.at[:, pl.ds(group * width, width)],
            kv_buf.at[which, group, space],
            own_sem.at[which, group],
        )

    for group in range(GROUPS):
        for which in range(2):
            own_copy(which, group).start()

    pl.semaphore_wait(barrier, chips + tm_count - 1)

    def direct(which, group, step):
        peer = lax.rem(chip + step, chips) * 2 + core
        source = (k_ref, v_ref)[which]
        return remote(
            source.at[:, pl.ds(group * width, width)],
            kv_buf.at[which, group, space],
            kv_send.at[which, group, step],
            kv_recv.at[which, group, step],
            "space",
            peer,
        )

    def direct_in(which, group, step):
        sender = lax.rem(chip - step + chips, chips) * 2 + core
        return remote(
            kv_buf.at[which, group, sender],
            kv_buf.at[which, group, sender],
            kv_send.at[which, group, step],
            kv_recv.at[which, group, step],
            "space",
            partner,
        )

    def to_partner(which, group, step):
        slot = lax.rem(chip - step + chips, chips) * 2 + core
        return remote(
            kv_buf.at[which, group, slot],
            kv_buf.at[which, group, slot],
            relay_send.at[which, group, step],
            relay_recv.at[which, group, step],
            "space",
            partner,
        )

    def from_partner(which, group, step):
        slot = lax.rem(chip - step + chips, chips) * 2 + 1 - core
        return remote(
            kv_buf.at[which, group, slot],
            kv_buf.at[which, group, slot],
            relay_send.at[which, group, step],
            relay_recv.at[which, group, step],
            "space",
            partner,
        )

    for group in range(GROUPS):
        for which in range(2):

            def send_chip(step, carry):
                direct(which, group, step).start()
                return carry

            lax.fori_loop(1, chips, send_chip, 0)
    for group in range(GROUPS):
        for which in range(2):
            own_copy(which, group).wait()
            to_partner(which, group, 0).start()

    size = tm_count * rows
    row = lax.broadcasted_iota(jnp.int32, (size, size), 0)
    col = lax.broadcasted_iota(jnp.int32, (size, size), 1)
    same = (row % rows == col % rows) & (col // rows <= row // rows)
    lower = same.astype(F32)
    steps = steps_ref[...]
    steps_t = jnp.transpose(steps)
    high = lax.Precision.HIGHEST
    total_rows = lax.dot_general(
        lower, steps, (((1,), (0,)), ((), ())), precision=high, preferred_element_type=F32
    )
    total_cols = lax.dot_general(
        steps_t, lower, (((1,), (1,)), ((), ())), precision=high, preferred_element_type=F32
    )
    for head in range(SHARED_HEADS):
        gap = total_cols[head : head + 1, :] - total_rows[:, head : head + 1]
        decay = jnp.exp(jnp.where(same, gap * rates_ref[head], -1e30))
        d_buf[head] = decay * steps_t[head : head + 1, :]

    block_of = lax.broadcasted_iota(jnp.int32, (1, space_count * tokens), 1) // tokens
    chosen = block_of == lists_ref[space, 0]
    for place in range(1, list_width):
        chosen = chosen | (block_of == lists_ref[space, place])
    bias = jnp.where(chosen, 0.0, -1e30).astype(F32)
    factor = math.log2(math.e) / math.sqrt(HEAD_DIM)

    def frame_out(group, step):
        peer = lax.rem(tm + step, tm_count)
        return remote(
            a_buf.at[group, peer],
            x_buf.at[group, tm],
            a_send.at[group, step],
            a_recv.at[group, step],
            "tm",
            peer,
        )

    def frame_in(group, step):
        sender = lax.rem(tm - step + tm_count, tm_count)
        return remote(
            a_buf.at[group, sender],
            x_buf.at[group, sender],
            a_send.at[group, step],
            a_recv.at[group, step],
            "tm",
            sender,
        )

    def own_frame(group):
        return pltpu.make_async_copy(
            a_buf.at[group, tm], x_buf.at[group, tm], self_sem.at[group]
        )

    for group in range(GROUPS):

        def relay(step, carry):
            for which in range(2):
                direct_in(which, group, step).wait_recv()
                to_partner(which, group, step).start()
            return carry

        def relayed(step, carry):
            for which in range(2):
                from_partner(which, group, step).wait_recv()
            return carry

        lax.fori_loop(1, chips, relay, 0)
        lax.fori_loop(0, chips, relayed, 0)
        for local in range(heads_here):
            lanes = slice(local * HEAD_DIM, (local + 1) * HEAD_DIM)
            head = group * heads_here + local
            query = q_ref[:, head * HEAD_DIM : (head + 1) * HEAD_DIM]
            key = kv_buf[0, group, :, :, lanes].reshape(space_count * tokens, HEAD_DIM)
            value = kv_buf[1, group, :, :, lanes].reshape(space_count * tokens, HEAD_DIM)
            scores = (
                lax.dot_general(
                    query, key, (((1,), (1,)), ((), ())), preferred_element_type=F32
                )
                * factor
                + bias
            )
            weights = jnp.exp2(scores - jnp.max(scores, axis=-1, keepdims=True))
            totals = jnp.sum(weights, axis=-1, keepdims=True)
            summed = jnp.dot(weights.astype(BF16), value, preferred_element_type=F32)
            attended = (summed / totals).reshape(tm_count, rows, HEAD_DIM)
            a_buf[group, :, :, lanes] = attended.astype(BF16)

        def send_frame(step, carry):
            frame_out(group, step).start()
            return carry

        lax.fori_loop(1, tm_count, send_frame, 0)
        own_frame(group).start()

    squares = jnp.zeros((size, 1), F32)
    for group in range(GROUPS):

        def take_frame(step, carry):
            frame_in(group, step).wait_recv()
            return carry

        lax.fori_loop(1, tm_count, take_frame, 0)
        own_frame(group).wait()
        part = x_buf[group].astype(F32).reshape(size, width)
        squares = squares + jnp.sum(part * part, axis=-1, keepdims=True)
    scale = lax.rsqrt(squares / channels + 1e-05)
    state = w_in_ref.shape[1]
    b_in = jnp.zeros((size, state), F32)
    c_out = jnp.zeros((size, state), F32)
    for group in range(GROUPS):
        span = slice(group * width, (group + 1) * width)
        part = x_buf[group].astype(F32).reshape(size, width)
        normed = (part * scale * pre_ref[:, span]).astype(BF16)
        n_buf[group] = normed
        b_in = b_in + jnp.dot(normed, w_in_ref[span, :], preferred_element_type=F32)
        c_out = c_out + jnp.dot(normed, w_out_ref[span, :], preferred_element_type=F32)
    gram = lax.dot_general(
        c_out, b_in, (((1,), (1,)), ((), ())), precision=high, preferred_element_type=F32
    )
    squares = jnp.zeros((size, 1), F32)
    for head in range(SHARED_HEADS):
        group, local = head // heads_here, head % heads_here
        lanes = slice(local * HEAD_DIM, (local + 1) * HEAD_DIM)
        values = n_buf[group, :, lanes]
        mixing = (gram * d_buf[head]).astype(BF16)
        mixed = jnp.dot(mixing, values, preferred_element_type=F32)
        mixed = mixed + skips_ref[head] * values.astype(F32)
        y_buf[:, head * HEAD_DIM : (head + 1) * HEAD_DIM] = mixed
        squares = squares + jnp.sum(mixed * mixed, axis=-1, keepdims=True)
    scale = lax.rsqrt(squares / channels + 1e-05)
    result = y_buf[...] * scale * post_ref[...]
    o_buf[...] = result.reshape(tm_count, rows, channels).astype(BF16)

    def result_out(step):
        peer = lax.rem(tm + step, tm_count)
        return remote(
            o_buf.at[peer], out_ref.at[tm], o_send.at[step], o_recv.at[step], "tm", peer
        )

    def result_in(step):
        sender = lax.rem(tm - step + tm_count, tm_count)
        return remote(
            o_buf.at[sender], out_ref.at[sender], o_send.at[step], o_recv.at[step], "tm", sender
        )

    def send_result(step, carry):
        result_out(step).start()
        return carry

    lax.fori_loop(1, tm_count, send_result, 0)
    own_result = pltpu.make_async_copy(o_buf.at[tm], out_ref.at[tm], self_sem.at[GROUPS])
    own_result.start()

    for group in range(GROUPS):

        def sent_chip(step, carry):
            for which in range(2):
                direct(which, group, step).wait_send()
            return carry

        def sent_partner(step, carry):
            for which in range(2):
                to_partner(which, group, step).wait_send()
            return carry

        def sent_frame(step, carry):
            frame_out(group, step).wait_send()
            return carry

        lax.fori_loop(1, chips, sent_chip, 0)
        lax.fori_loop(0, chips, sent_partner, 0)
        lax.fori_loop(1, tm_count, sent_frame, 0)

    def finish(step, carry):
        result_out(step).wait_send()
        result_in(step).wait_recv()
        return carry

    own_result.wait()
    lax.fori_loop(1, tm_count, finish, 0)


def body(
    queries,
    key_vectors,
    value_vectors,
    block_lists,
    step_sizes,
    decay_rates,
    skip_gains,
    pre_gain,
    state_in_weight,
    state_out_weight,
    post_gain,
):
    tokens, channels = queries.shape[1], queries.shape[2]
    space_count = lax.axis_size("space")
    tm_count = lax.axis_size("tm")
    rows = tokens // tm_count
    width = channels // GROUPS
    chips = space_count // 2
    size = tokens
    vmem = pl.BlockSpec(memory_space=pltpu.VMEM)
    smem = pl.BlockSpec(memory_space=pltpu.SMEM)
    hbm = pl.BlockSpec(memory_space=pl.ANY)
    dma = pltpu.SemaphoreType.DMA
    out = pl.pallas_call(
        functools.partial(kernel, (space_count, tm_count, block_lists.shape[1])),
        out_shape=jax.ShapeDtypeStruct((tm_count, rows, channels), BF16),
        in_specs=[smem, smem, smem, vmem, hbm, hbm, vmem, vmem, vmem, vmem, vmem],
        out_specs=hbm,
        scratch_shapes=[
            pltpu.VMEM((2, GROUPS, space_count, tokens, width), BF16),
            pltpu.VMEM((GROUPS, tm_count, rows, width), BF16),
            pltpu.VMEM((GROUPS, tm_count, rows, width), BF16),
            pltpu.VMEM((GROUPS, size, width), BF16),
            pltpu.VMEM((size, channels), F32),
            pltpu.VMEM((tm_count, rows, channels), BF16),
            pltpu.VMEM((SHARED_HEADS, size, size), F32),
            dma((2, GROUPS)),
            dma((2, GROUPS, chips)),
            dma((2, GROUPS, chips)),
            dma((2, GROUPS, chips)),
            dma((2, GROUPS, chips)),
            dma((GROUPS, tm_count)),
            dma((GROUPS, tm_count)),
            dma((tm_count,)),
            dma((tm_count,)),
            dma((GROUPS + 1,)),
        ],
        compiler_params=pltpu.CompilerParams(
            collective_id=0, has_side_effects=True, vmem_limit_bytes=50 * 1024 * 1024
        ),
        name="attend_and_mix",
    )(
        block_lists,
        decay_rates,
        skip_gains,
        queries.reshape(tokens, channels),
        key_vectors.reshape(tokens, channels),
        value_vectors.reshape(tokens, channels),
        step_sizes.reshape(size, SHARED_HEADS),
        pre_gain.reshape(1, channels),
        state_in_weight,
        state_out_weight,
        post_gain.reshape(1, channels),
    )
    return out.reshape(1, tokens, channels)


def solution(mesh):
    placed = (
        P("tm", "space", None),
        P("tm", "space", None),
        P("tm", "space", None),
        P(),
        P(None, ("space", "tm"), None),
        P(),
        P(),
        P(),
        P(),
        P(),
        P(),
    )
    return jax.shard_map(
        body, mesh=mesh, in_specs=placed, out_specs=P("tm", "space", None), check_vma=False
    )
```

time: 111 us -> 58.9 us (0.53)
  the two profiles are of different devices: /device:TPU:0 before, /device:TPU:11 now
where the time goes in v1:
time: 58.9 us; the launch traced here: 58.5 us
  Pallas kernels  50.9 us (86%)
  local copies, waits for them, and re-layouts  7.62 us (13%)
    pallas_call x1, Pallas kernels, body(): pl.pallas_call(functools.partial(kernel, (space_count, tm_count, block_li...  50.9 us
    unnamed x21, local copies, waits for them, and re-layouts  7.62 us

profile of v1, /device:TPU:11, one launch (start us, length us, event | category | flops | bytes accessed | tf_op | source)
XLA Modules:
  0.0 58.5 jit_solution(7641116032849022533)
XLA Ops:
  0.0 0.0 copy-start.1
  0.0 0.0 copy-start.2
  0.0 1.3 %copy.12.w_in_ref = bf16[2048,64]{1,0:T(8,128)(2,1)S(1)} copy(bf16[2048,64]{0,1:T(8,128)(2,1)} %param.19) | data formatting | bytes 524288 | tf_op args[8]
  1.3 0.0 copy-start
  1.3 1.3 %copy.13.w_out_ref = bf16[2048,64]{1,0:T(8,128)(2,1)S(1)} copy(bf16[2048,64]{0,1:T(8,128)(2,1)} %param.20) | data formatting | bytes 524288 | tf_op args[9]
  2.6 0.0 copy-done.1
  2.6 0.0 copy-done.2
  2.6 0.0 copy-done
  2.6 0.0 copy-start.3
  2.7 0.8 %copy-done.3 = f32[8,16,16]{2,1,0:T(8,128)S(1)} copy-done((f32[8,16,16]{2,1,0:T(8,128)S(1)}, f32[8,16,16]{2,1,0:T(8,128)}, u32[]{:S(2)}) %copy-start.3) | copy-done | bytes 8216
  3.5 0.0 copy-start.4
  3.5 0.7 %copy-done.4 = f32[2048]{0:T(1024)S(1)} copy-done((f32[2048]{0:T(1024)S(1)}, f32[2048]{0:T(1024)}, u32[]{:S(2)}) %copy-start.4) | copy-done | bytes 8216
  4.2 0.0 copy-start.5
  4.2 0.7 %copy-done.5 = f32[2048]{0:T(1024)S(1)} copy-done((f32[2048]{0:T(1024)S(1)}, f32[2048]{0:T(1024)}, u32[]{:S(2)}) %copy-start.5) | copy-done | bytes 8216
  4.9 0.0 copy-start.6
  4.9 0.7 %copy-done.6 = s32[4,3]{1,0:T(4,128)S(1)} copy-done((s32[4,3]{1,0:T(4,128)S(1)}, s32[4,3]{1,0:T(4,128)}, u32[]{:S(2)}) %copy-start.6) | copy-done | bytes 72
  5.6 0.0 copy-start.7
  5.6 0.7 %copy-done.7 = f32[16]{0:T(128)S(1)} copy-done((f32[16]{0:T(128)S(1)}, f32[16]{0:T(128)}, u32[]{:S(2)}) %copy-start.7) | copy-done | bytes 88
  6.2 0.0 copy-start.8
  6.2 0.7 %copy-done.8 = f32[16]{0:T(128)S(1)} copy-done((f32[16]{0:T(128)S(1)}, f32[16]{0:T(128)}, u32[]{:S(2)}) %copy-start.8) | copy-done | bytes 88
  6.9 50.9 %attend_and_mix.1 = bf16[8,16,2048]{2,1,0:T(8,128)(2,1)S(1)} custom-call(s32[4,3]{1,0:T(4,128)S(1)} %copy-done.6, f32[16]{0:T(128)S(1)} %copy-done.7, f32[16]{0:T(128)S(1)} %copy-done.8, bf16[128,2048]{1,0:T(8,128)(2,1)S(1)} %bitcast.8, bf16[128,2048]{1,0:T(8,128)(2,1)S(1)} %bitcast.9, bf16[128,2048]{1,0:T(8,128)(2,1)S(1)} %bitcast.10, ...), custom_call_target="tpu_custom_call" | custom-call | tf_op jit(solution)/shard_map/attend_and_mix/pallas_call | solution.py:369
  57.8 0.8 %copy.15 = bf16[1,128,2048]{2,1,0:T(8,128)(2,1)} copy(bf16[1,128,2048]{2,1,0:T(8,128)(2,1)S(1)} %bitcast.7) | data formatting | bytes 1048576
Async XLA Ops:
  0.0 2.6 %copy-start.1 = (bf16[1,128,2048]{2,1,0:T(8,128)(2,1)S(1)}, bf16[1,128,2048]{2,1,0:T(8,128)(2,1)}, u32[]{:S(2)}) copy-start(bf16[1,128,2048]{2,1,0:T(8,128)(2,1)} %param.12) | copy-start | bytes 1572868
  0.0 2.6 %copy-start.2 = (bf16[1,128,2048]{2,1,0:T(8,128)(2,1)S(1)}, bf16[1,128,2048]{2,1,0:T(8,128)(2,1)}, u32[]{:S(2)}) copy-start(bf16[1,128,2048]{2,1,0:T(8,128)(2,1)} %param.13) | copy-start | bytes 1572868
  1.3 1.3 %copy-start = (bf16[1,128,2048]{2,1,0:T(8,128)(2,1)S(1)}, bf16[1,128,2048]{2,1,0:T(8,128)(2,1)}, u32[]{:S(2)}) copy-start(bf16[1,128,2048]{2,1,0:T(8,128)(2,1)} %param.11) | copy-start | bytes 1572868
  2.6 0.8 %copy-start.3 = (f32[8,16,16]{2,1,0:T(8,128)S(1)}, f32[8,16,16]{2,1,0:T(8,128)}, u32[]{:S(2)}) copy-start(f32[8,16,16]{2,1,0:T(8,128)} %param.15) | copy-start | bytes 24580
  3.5 0.7 %copy-start.4 = (f32[2048]{0:T(1024)S(1)}, f32[2048]{0:T(1024)}, u32[]{:S(2)}) copy-start(f32[2048]{0:T(1024)} %param.18) | copy-start | bytes 24580
  4.2 0.7 %copy-start.5 = (f32[2048]{0:T(1024)S(1)}, f32[2048]{0:T(1024)}, u32[]{:S(2)}) copy-start(f32[2048]{0:T(1024)} %param.21) | copy-start | bytes 24580
  4.9 0.7 %copy-start.6 = (s32[4,3]{1,0:T(4,128)S(1)}, s32[4,3]{1,0:T(4,128)}, u32[]{:S(2)}) copy-start(s32[4,3]{1,0:T(4,128)} %lists_ref.1) | copy-start | bytes 148
  5.6 0.7 %copy-start.7 = (f32[16]{0:T(128)S(1)}, f32[16]{0:T(128)}, u32[]{:S(2)}) copy-start(f32[16]{0:T(128)} %rates_ref.1) | copy-start | bytes 196
  6.2 0.7 %copy-start.8 = (f32[16]{0:T(128)S(1)}, f32[16]{0:T(128)}, u32[]{:S(2)}) copy-start(f32[16]{0:T(128)} %skips_ref.1) | copy-start | bytes 196

commit v2 on v1

--- a/solution.py
+++ b/solution.py
@@ -12,6 +12,7 @@
 HEAD_DIM = 128
 BLOCK = 128
 GROUPS = 4
+VMEM_BYTES = 63 * 1024 * 1024
 MESH = pl.DeviceIdType.MESH
 F32 = jnp.float32
 BF16 = jnp.bfloat16
@@ -30,18 +31,28 @@
 
 def kernel(
     dims,
+    lists_hbm,
+    rates_hbm,
+    skips_hbm,
+    q_hbm,
+    k_ref,
+    v_ref,
+    steps_hbm,
+    pre_hbm,
+    w_in_hbm,
+    w_out_hbm,
+    post_hbm,
+    out_ref,
     lists_ref,
     rates_ref,
     skips_ref,
     q_ref,
-    k_ref,
-    v_ref,
     steps_ref,
     pre_ref,
     w_in_ref,
     w_out_ref,
     post_ref,
-    out_ref,
+    load_sem,
     kv_buf,
     a_buf,
     x_buf,
@@ -61,7 +72,7 @@
     self_sem,
 ):
     space_count, tm_count, list_width = dims
-    tokens, channels = q_ref.shape
+    tokens, channels = q_hbm.shape
     rows = tokens // tm_count
     width = channels // GROUPS
     heads_here = width // HEAD_DIM
@@ -100,6 +111,25 @@
         for which in range(2):
             own_copy(which, group).start()
 
+    loads = [
+        pltpu.make_async_copy(source, target, load_sem.at[place])
+        for place, (source, target) in enumerate(
+            (
+                (steps_hbm, steps_ref),
+                (rates_hbm, rates_ref),
+                (lists_hbm, lists_ref),
+                (q_hbm, q_ref),
+                (skips_hbm, skips_ref),
+                (pre_hbm, pre_ref),
+                (w_in_hbm, w_in_ref),
+                (w_out_hbm, w_out_ref),
+                (post_hbm, post_ref),
+            )
+        )
+    ]
+    for load in loads:
+        load.start()
+
     pl.semaphore_wait(barrier, chips + tm_count - 1)
 
     def direct(which, group, step):
@@ -159,6 +189,9 @@
         for which in range(2):
             own_copy(which, group).wait()
             to_partner(which, group, 0).start()
+
+    for load in loads:
+        load.wait()
 
     size = tm_count * rows
     row = lax.broadcasted_iota(jnp.int32, (size, size), 0)
@@ -266,7 +299,7 @@
         part = x_buf[group].astype(F32).reshape(size, width)
         squares = squares + jnp.sum(part * part, axis=-1, keepdims=True)
     scale = lax.rsqrt(squares / channels + 1e-05)
-    state = w_in_ref.shape[1]
+    state = w_in_ref.shape[0]
     b_in = jnp.zeros((size, state), F32)
     c_out = jnp.zeros((size, state), F32)
     for group in range(GROUPS):
@@ -274,8 +307,13 @@
         part = x_buf[group].astype(F32).reshape(size, width)
         normed = (part * scale * pre_ref[:, span]).astype(BF16)
         n_buf[group] = normed
-        b_in = b_in + jnp.dot(normed, w_in_ref[span, :], preferred_element_type=F32)
-        c_out = c_out + jnp.dot(normed, w_out_ref[span, :], preferred_element_type=F32)
+        across = (((1,), (1,)), ((), ()))
+        b_in = b_in + lax.dot_general(
+            normed, w_in_ref[:, span], across, preferred_element_type=F32
+        )
+        c_out = c_out + lax.dot_general(
+            normed, w_out_ref[:, span], across, preferred_element_type=F32
+        )
     gram = lax.dot_general(
         c_out, b_in, (((1,), (1,)), ((), ())), precision=high, preferred_element_type=F32
     )
@@ -362,16 +400,25 @@
     width = channels // GROUPS
     chips = space_count // 2
     size = tokens
-    vmem = pl.BlockSpec(memory_space=pltpu.VMEM)
-    smem = pl.BlockSpec(memory_space=pltpu.SMEM)
+    state = state_in_weight.shape[1]
     hbm = pl.BlockSpec(memory_space=pl.ANY)
     dma = pltpu.SemaphoreType.DMA
     out = pl.pallas_call(
         functools.partial(kernel, (space_count, tm_count, block_lists.shape[1])),
         out_shape=jax.ShapeDtypeStruct((tm_count, rows, channels), BF16),
-        in_specs=[smem, smem, smem, vmem, hbm, hbm, vmem, vmem, vmem, vmem, vmem],
+        in_specs=[hbm] * 11,
         out_specs=hbm,
         scratch_shapes=[
+            pltpu.SMEM(block_lists.shape, jnp.int32),
+            pltpu.SMEM(decay_rates.shape, F32),
+            pltpu.SMEM(skip_gains.shape, F32),
+            pltpu.VMEM((tokens, channels), BF16),
+            pltpu.VMEM((size, SHARED_HEADS), F32),
+            pltpu.VMEM((1, channels), F32),
+            pltpu.VMEM((state, channels), BF16),
+            pltpu.VMEM((state, channels), BF16),
+            pltpu.VMEM((1, channels), F32),
+            dma((9,)),
             pltpu.VMEM((2, GROUPS, space_count, tokens, width), BF16),
             pltpu.VMEM((GROUPS, tm_count, rows, width), BF16),
             pltpu.VMEM((GROUPS, tm_count, rows, width), BF16),
@@ -391,7 +438,7 @@
             dma((GROUPS + 1,)),
         ],
         compiler_params=pltpu.CompilerParams(
-            collective_id=0, has_side_effects=True, vmem_limit_bytes=50 * 1024 * 1024
+            collective_id=0, has_side_effects=True, vmem_limit_bytes=VMEM_BYTES
         ),
         name="attend_and_mix",
     )(
@@ -403,8 +450,8 @@
         value_vectors.reshape(tokens, channels),
         step_sizes.reshape(size, SHARED_HEADS),
         pre_gain.reshape(1, channels),
-        state_in_weight,
-        state_out_weight,
+        state_in_weight.T,
+        state_out_weight.T,
         post_gain.reshape(1, channels),
     )
     return out.reshape(1, tokens, channels)

time: 58.9 us -> 52.7 us (0.89)
  local copies, waits for them, and re-layouts: 7.62 us -> 1.88 us
    unnamed x21 -> x1, local copies, waits for them, and re-layouts: 7.62 us -> 1.88 us
where the time goes in v2:
time: 52.7 us; the launch traced here: 52.6 us
  Pallas kernels  50.7 us (96%)
  local copies, waits for them, and re-layouts  1.88 us (4%)
    pallas_call x1, Pallas kernels, body(): pl.pallas_call(functools.partial(kernel, (space_count, tm_count, block_li...  50.7 us
    unnamed x1, local copies, waits for them, and re-layouts  1.88 us

profile of v2, /device:TPU:11, one launch (start us, length us, event | category | flops | bytes accessed | tf_op | source)
XLA Modules:
  0.0 52.6 jit_solution(6716567315697039696)
XLA Ops:
  0.0 50.7 %attend_and_mix.1 = bf16[8,16,2048]{2,1,0:T(8,128)(2,1)} custom-call(s32[4,3]{1,0:T(4,128)} %lists_hbm.1, f32[16]{0:T(128)} %rates_hbm.1, f32[16]{0:T(128)} %skips_hbm.1, bf16[128,2048]{1,0:T(8,128)(2,1)} %bitcast.10, bf16[128,2048]{1,0:T(8,128)(2,1)} %bitcast.11, bf16[128,2048]{1,0:T(8,128)(2,1)} %bitcast.12, f32[128,16]{1,0:T(8,128)} %bitcast.15, ...), custom_call_target="tpu_custom_call" | custom-call | tf_op jit(solution)/shard_map/attend_and_mix/pallas_call | solution.py:406
  50.7 1.9 %copy.13 = bf16[1,128,2048]{2,1,0:T(8,128)(2,1)} copy(bf16[1,128,2048]{2,1,0:T(8,128)(2,1)} %bitcast.9) | data formatting | bytes 1048576

commit v3 on v2

--- a/solution.py
+++ b/solution.py
@@ -11,7 +11,7 @@
 SHARED_HEADS = 16
 HEAD_DIM = 128
 BLOCK = 128
-GROUPS = 4
+GROUPS = 8
 VMEM_BYTES = 63 * 1024 * 1024
 MESH = pl.DeviceIdType.MESH
 F32 = jnp.float32
@@ -53,6 +53,9 @@
     w_out_ref,
     post_ref,
     load_sem,
+    step_send,
+    step_recv,
+    step_own,
     kv_buf,
     a_buf,
     x_buf,
@@ -67,18 +70,23 @@
     relay_recv,
     a_send,
     a_recv,
+    l_send,
+    l_recv,
     o_send,
     o_recv,
     self_sem,
 ):
     space_count, tm_count, list_width = dims
     tokens, channels = q_hbm.shape
-    rows = tokens // tm_count
+    half_count = tm_count // 2
+    rows = tokens // half_count
     width = channels // GROUPS
     heads_here = width // HEAD_DIM
     chips = space_count // 2
     space = lax.axis_index("space")
     tm = lax.axis_index("tm")
+    half = tm // half_count
+    place = tm % half_count
     chip = space // 2
     core = space % 2
     partner = chip * 2 + 1 - core
@@ -112,10 +120,9 @@
             own_copy(which, group).start()
 
     loads = [
-        pltpu.make_async_copy(source, target, load_sem.at[place])
-        for place, (source, target) in enumerate(
+        pltpu.make_async_copy(source, target, load_sem.at[index])
+        for index, (source, target) in enumerate(
             (
-                (steps_hbm, steps_ref),
                 (rates_hbm, rates_ref),
                 (lists_hbm, lists_ref),
                 (q_hbm, q_ref),
@@ -177,6 +184,29 @@
             partner,
         )
 
+    def step_copy(which, target, part):
+        return remote(
+            steps_hbm,
+            steps_ref.at[:, part],
+            step_send.at[which],
+            step_recv.at[part],
+            "tm",
+            target,
+        )
+
+    def step_arrival(part, origin):
+        return remote(
+            steps_hbm,
+            steps_ref.at[:, part],
+            step_send.at[0],
+            step_recv.at[part],
+            "tm",
+            origin,
+        )
+
+    def step_local(part):
+        return pltpu.make_async_copy(steps_hbm, steps_ref.at[:, part], step_own.at[part])
+
     for group in range(GROUPS):
         for which in range(2):
 
@@ -190,60 +220,112 @@
             own_copy(which, group).wait()
             to_partner(which, group, 0).start()
 
+    for which in range(2):
+        target = which * half_count + tm // 2
+        part = tm % 2
+
+        @pl.when(target != tm)
+        def _():
+            step_copy(which, target, part).start()
+
+        @pl.when(target == tm)
+        def _():
+            step_local(part).start()
+
     for load in loads:
         load.wait()
-
-    size = tm_count * rows
-    row = lax.broadcasted_iota(jnp.int32, (size, size), 0)
-    col = lax.broadcasted_iota(jnp.int32, (size, size), 1)
+    for part in range(2):
+        origin = 2 * place + part
+
+        @pl.when(origin != tm)
+        def _():
+            step_arrival(part, origin).wait_recv()
+
+        @pl.when(origin == tm)
+        def _():
+            step_local(part).wait()
+
+    size = half_count * rows
+    row = lax.broadcasted_iota(jnp.int32, (2 * size, 2 * size), 0)
+    col = lax.broadcasted_iota(jnp.int32, (2 * size, 2 * size), 1)
     same = (row % rows == col % rows) & (col // rows <= row // rows)
     lower = same.astype(F32)
-    steps = steps_ref[...]
+    steps = steps_ref[...].reshape(2 * size, SHARED_HEADS)
+    swapped = jnp.concatenate([steps[size:], steps[:size]], axis=0)
+    steps = jnp.where(half == 1, steps, swapped)
     steps_t = jnp.transpose(steps)
     high = lax.Precision.HIGHEST
     total_rows = lax.dot_general(
-        lower, steps, (((1,), (0,)), ((), ())), precision=high, preferred_element_type=F32
+        lower[size:], steps, (((1,), (0,)), ((), ())), precision=high, preferred_element_type=F32
     )
     total_cols = lax.dot_general(
         steps_t, lower, (((1,), (1,)), ((), ())), precision=high, preferred_element_type=F32
     )
+    first = (1 - half) * size
+    counts = (lower[size:] > 0.5) & (col[size:] >= first)
     for head in range(SHARED_HEADS):
         gap = total_cols[head : head + 1, :] - total_rows[:, head : head + 1]
-        decay = jnp.exp(jnp.where(same, gap * rates_ref[head], -1e30))
+        decay = jnp.exp(jnp.where(counts, gap * rates_ref[head], -1e30))
         d_buf[head] = decay * steps_t[head : head + 1, :]
+
+    @pl.when(half == 0)
+    def _():
+        x_buf[:, 0:half_count] = jnp.zeros((GROUPS, half_count, rows, width), BF16)
 
     block_of = lax.broadcasted_iota(jnp.int32, (1, space_count * tokens), 1) // tokens
     chosen = block_of == lists_ref[space, 0]
-    for place in range(1, list_width):
-        chosen = chosen | (block_of == lists_ref[space, place])
+    for entry in range(1, list_width):
+        chosen = chosen | (block_of == lists_ref[space, entry])
     bias = jnp.where(chosen, 0.0, -1e30).astype(F32)
     factor = math.log2(math.e) / math.sqrt(HEAD_DIM)
 
     def frame_out(group, step):
-        peer = lax.rem(tm + step, tm_count)
+        peer = lax.rem(place + step, half_count)
         return remote(
             a_buf.at[group, peer],
-            x_buf.at[group, tm],
+            x_buf.at[group, half_count + place],
             a_send.at[group, step],
             a_recv.at[group, step],
             "tm",
-            peer,
+            half * half_count + peer,
         )
 
     def frame_in(group, step):
-        sender = lax.rem(tm - step + tm_count, tm_count)
+        sender = lax.rem(place - step + half_count, half_count)
+        return remote(
+            a_buf.at[group, sender],
+            x_buf.at[group, half_count + sender],
+            a_send.at[group, step],
+            a_recv.at[group, step],
+            "tm",
+            half * half_count + sender,
+        )
+
+    def later_out(group, step):
+        peer = lax.rem(place + step, half_count)
+        return remote(
+            a_buf.at[group, peer],
+            x_buf.at[group, place],
+            l_send.at[group, step],
+            l_recv.at[group, step],
+            "tm",
+            half_count + peer,
+        )
+
+    def earlier_in(group, step):
+        sender = lax.rem(place - step + half_count, half_count)
         return remote(
             a_buf.at[group, sender],
             x_buf.at[group, sender],
-            a_send.at[group, step],
-            a_recv.at[group, step],
+            l_send.at[group, step],
+            l_recv.at[group, step],
             "tm",
             sender,
         )
 
     def own_frame(group):
         return pltpu.make_async_copy(
-            a_buf.at[group, tm], x_buf.at[group, tm], self_sem.at[group]
+            a_buf.at[group, place], x_buf.at[group, half_count + place], self_sem.at[group]
         )
 
     for group in range(GROUPS):
@@ -277,46 +359,61 @@
             weights = jnp.exp2(scores - jnp.max(scores, axis=-1, keepdims=True))
             totals = jnp.sum(weights, axis=-1, keepdims=True)
             summed = jnp.dot(weights.astype(BF16), value, preferred_element_type=F32)
-            attended = (summed / totals).reshape(tm_count, rows, HEAD_DIM)
+            attended = (summed / totals).reshape(half_count, rows, HEAD_DIM)
             a_buf[group, :, :, lanes] = attended.astype(BF16)
 
         def send_frame(step, carry):
             frame_out(group, step).start()
             return carry
 
-        lax.fori_loop(1, tm_count, send_frame, 0)
+        def send_later(step, carry):
+            later_out(group, step).start()
+            return carry
+
+        @pl.when(half == 0)
+        def _():
+            lax.fori_loop(0, half_count, send_later, 0)
+
+        lax.fori_loop(1, half_count, send_frame, 0)
         own_frame(group).start()
 
-    squares = jnp.zeros((size, 1), F32)
+    squares = jnp.zeros((2 * size, 1), F32)
     for group in range(GROUPS):
 
         def take_frame(step, carry):
             frame_in(group, step).wait_recv()
             return carry
 
-        lax.fori_loop(1, tm_count, take_frame, 0)
+        def take_earlier(step, carry):
+            earlier_in(group, step).wait_recv()
+            return carry
+
+        lax.fori_loop(1, half_count, take_frame, 0)
         own_frame(group).wait()
-        part = x_buf[group].astype(F32).reshape(size, width)
+
+        @pl.when(half == 1)
+        def _():
+            lax.fori_loop(0, half_count, take_earlier, 0)
+
+        part = x_buf[group].astype(F32).reshape(2 * size, width)
         squares = squares + jnp.sum(part * part, axis=-1, keepdims=True)
     scale = lax.rsqrt(squares / channels + 1e-05)
     state = w_in_ref.shape[0]
-    b_in = jnp.zeros((size, state), F32)
+    b_in = jnp.zeros((2 * size, state), F32)
     c_out = jnp.zeros((size, state), F32)
+    across = (((1,), (1,)), ((), ()))
     for group in range(GROUPS):
         span = slice(group * width, (group + 1) * width)
-        part = x_buf[group].astype(F32).reshape(size, width)
+        part = x_buf[group].astype(F32).reshape(2 * size, width)
         normed = (part * scale * pre_ref[:, span]).astype(BF16)
         n_buf[group] = normed
-        across = (((1,), (1,)), ((), ()))
         b_in = b_in + lax.dot_general(
             normed, w_in_ref[:, span], across, preferred_element_type=F32
         )
         c_out = c_out + lax.dot_general(
-            normed, w_out_ref[:, span], across, preferred_element_type=F32
-        )
-    gram = lax.dot_general(
-        c_out, b_in, (((1,), (1,)), ((), ())), precision=high, preferred_element_type=F32
-    )
+            normed[size:], w_out_ref[:, span], across, preferred_element_type=F32
+        )
+    gram = lax.dot_general(c_out, b_in, across, precision=high, preferred_element_type=F32)
     squares = jnp.zeros((size, 1), F32)
     for head in range(SHARED_HEADS):
         group, local = head // heads_here, head % heads_here
@@ -324,31 +421,41 @@
         values = n_buf[group, :, lanes]
         mixing = (gram * d_buf[head]).astype(BF16)
         mixed = jnp.dot(mixing, values, preferred_element_type=F32)
-        mixed = mixed + skips_ref[head] * values.astype(F32)
+        mixed = mixed + skips_ref[head] * values[size:].astype(F32)
         y_buf[:, head * HEAD_DIM : (head + 1) * HEAD_DIM] = mixed
         squares = squares + jnp.sum(mixed * mixed, axis=-1, keepdims=True)
     scale = lax.rsqrt(squares / channels + 1e-05)
     result = y_buf[...] * scale * post_ref[...]
-    o_buf[...] = result.reshape(tm_count, rows, channels).astype(BF16)
+    o_buf[...] = result.reshape(half_count, rows, channels).astype(BF16)
 
     def result_out(step):
-        peer = lax.rem(tm + step, tm_count)
-        return remote(
-            o_buf.at[peer], out_ref.at[tm], o_send.at[step], o_recv.at[step], "tm", peer
+        peer = lax.rem(place + step, half_count)
+        return remote(
+            o_buf.at[peer],
+            out_ref.at[place],
+            o_send.at[step],
+            o_recv.at[step],
+            "tm",
+            half * half_count + peer,
         )
 
     def result_in(step):
-        sender = lax.rem(tm - step + tm_count, tm_count)
-        return remote(
-            o_buf.at[sender], out_ref.at[sender], o_send.at[step], o_recv.at[step], "tm", sender
+        sender = lax.rem(place - step + half_count, half_count)
+        return remote(
+            o_buf.at[sender],
+            out_ref.at[sender],
+            o_send.at[step],
+            o_recv.at[step],
+            "tm",
+            half * half_count + sender,
         )
 
     def send_result(step, carry):
         result_out(step).start()
         return carry
 
-    lax.fori_loop(1, tm_count, send_result, 0)
-    own_result = pltpu.make_async_copy(o_buf.at[tm], out_ref.at[tm], self_sem.at[GROUPS])
+    lax.fori_loop(1, half_count, send_result, 0)
+    own_result = pltpu.make_async_copy(o_buf.at[place], out_ref.at[place], self_sem.at[GROUPS])
     own_result.start()
 
     for group in range(GROUPS):
@@ -369,7 +476,23 @@
 
         lax.fori_loop(1, chips, sent_chip, 0)
         lax.fori_loop(0, chips, sent_partner, 0)
-        lax.fori_loop(1, tm_count, sent_frame, 0)
+        lax.fori_loop(1, half_count, sent_frame, 0)
+
+        def sent_later(step, carry):
+            later_out(group, step).wait_send()
+            return carry
+
+        @pl.when(half == 0)
+        def _():
+            lax.fori_loop(0, half_count, sent_later, 0)
+
+    for which in range(2):
+        target = which * half_count + tm // 2
+
+        @pl.when(target != tm)
+        def _():
+            step_copy(which, target, tm % 2).wait_send()
+
 
     def finish(step, carry):
         result_out(step).wait_send()
@@ -377,7 +500,7 @@
         return carry
 
     own_result.wait()
-    lax.fori_loop(1, tm_count, finish, 0)
+    lax.fori_loop(1, half_count, finish, 0)
 
 
 def body(
@@ -396,7 +519,8 @@
     tokens, channels = queries.shape[1], queries.shape[2]
     space_count = lax.axis_size("space")
     tm_count = lax.axis_size("tm")
-    rows = tokens // tm_count
+    half_count = tm_count // 2
+    rows = tokens // half_count
     width = channels // GROUPS
     chips = space_count // 2
     size = tokens
@@ -405,7 +529,7 @@
     dma = pltpu.SemaphoreType.DMA
     out = pl.pallas_call(
         functools.partial(kernel, (space_count, tm_count, block_lists.shape[1])),
-        out_shape=jax.ShapeDtypeStruct((tm_count, rows, channels), BF16),
+        out_shape=jax.ShapeDtypeStruct((half_count, rows, channels), BF16),
         in_specs=[hbm] * 11,
         out_specs=hbm,
         scratch_shapes=[
@@ -413,28 +537,33 @@
             pltpu.SMEM(decay_rates.shape, F32),
             pltpu.SMEM(skip_gains.shape, F32),
             pltpu.VMEM((tokens, channels), BF16),
-            pltpu.VMEM((size, SHARED_HEADS), F32),
+            pltpu.VMEM((tm_count, 2, tokens // tm_count, SHARED_HEADS), F32),
             pltpu.VMEM((1, channels), F32),
             pltpu.VMEM((state, channels), BF16),
             pltpu.VMEM((state, channels), BF16),
             pltpu.VMEM((1, channels), F32),
-            dma((9,)),
+            dma((8,)),
+            dma((2,)),
+            dma((2,)),
+            dma((2,)),
             pltpu.VMEM((2, GROUPS, space_count, tokens, width), BF16),
+            pltpu.VMEM((GROUPS, half_count, rows, width), BF16),
             pltpu.VMEM((GROUPS, tm_count, rows, width), BF16),
-            pltpu.VMEM((GROUPS, tm_count, rows, width), BF16),
-            pltpu.VMEM((GROUPS, size, width), BF16),
+            pltpu.VMEM((GROUPS, 2 * size, width), BF16),
             pltpu.VMEM((size, channels), F32),
-            pltpu.VMEM((tm_count, rows, channels), BF16),
-            pltpu.VMEM((SHARED_HEADS, size, size), F32),
+            pltpu.VMEM((half_count, rows, channels), BF16),
+            pltpu.VMEM((SHARED_HEADS, size, 2 * size), F32),
             dma((2, GROUPS)),
             dma((2, GROUPS, chips)),
             dma((2, GROUPS, chips)),
             dma((2, GROUPS, chips)),
             dma((2, GROUPS, chips)),
-            dma((GROUPS, tm_count)),
-            dma((GROUPS, tm_count)),
-            dma((tm_count,)),
-            dma((tm_count,)),
+            dma((GROUPS, half_count)),
+            dma((GROUPS, half_count)),
+            dma((GROUPS, half_count)),
+            dma((GROUPS, half_count)),
+            dma((half_count,)),
+            dma((half_count,)),
             dma((GROUPS + 1,)),
         ],
         compiler_params=pltpu.CompilerParams(
@@ -448,7 +577,7 @@
         queries.reshape(tokens, channels),
         key_vectors.reshape(tokens, channels),
         value_vectors.reshape(tokens, channels),
-        step_sizes.reshape(size, SHARED_HEADS),
+        step_sizes,
         pre_gain.reshape(1, channels),
         state_in_weight.T,
         state_out_weight.T,

time: 52.7 us -> 49.6 us (0.941)
  the two profiles are of different devices: /device:TPU:11 before, /device:TPU:0 now
where the time goes in v3:
time: 49.6 us; the launch traced here: 49 us
  Pallas kernels  47.2 us (95%)
  local copies, waits for them, and re-layouts  1.88 us (4%)
    pallas_call x1, Pallas kernels, body(): pl.pallas_call(functools.partial(kernel, (space_count, tm_count, block_li...  47.2 us
    unnamed x1, local copies, waits for them, and re-layouts  1.88 us

profile of v3, /device:TPU:0, one launch (start us, length us, event | category | flops | bytes accessed | tf_op | source)
XLA Modules:
  0.0 49.0 jit_solution(14910425438114693185)
XLA Ops:
  0.0 47.2 %attend_and_mix.1 = bf16[4,32,2048]{2,1,0:T(8,128)(2,1)} custom-call(s32[4,3]{1,0:T(4,128)} %lists_hbm.1, f32[16]{0:T(128)} %rates_hbm.1, f32[16]{0:T(128)} %skips_hbm.1, bf16[128,2048]{1,0:T(8,128)(2,1)} %bitcast.9, bf16[128,2048]{1,0:T(8,128)(2,1)} %bitcast.10, bf16[128,2048]{1,0:T(8,128)(2,1)} %bitcast.11, f32[8,16,16]{2,1,0:T(8,128)} %steps_hbm.1, ...), custom_call_target="tpu_custom_call" | custom-call | tf_op jit(solution)/shard_map/attend_and_mix/pallas_call | solution.py:530
  47.2 1.9 %copy.13 = bf16[1,128,2048]{2,1,0:T(8,128)(2,1)} copy(bf16[1,128,2048]{2,1,0:T(8,128)(2,1)} %bitcast.8) | data formatting | bytes 1048576

commit v4 on v3

--- a/solution.py
+++ b/solution.py
@@ -12,6 +12,7 @@
 HEAD_DIM = 128
 BLOCK = 128
 GROUPS = 8
+LAG = 3
 VMEM_BYTES = 63 * 1024 * 1024
 MESH = pl.DeviceIdType.MESH
 F32 = jnp.float32
@@ -111,7 +112,7 @@
         source = (k_ref, v_ref)[which]
         return pltpu.make_async_copy(
             source.at[:, pl.ds(group * width, width)],
-            kv_buf.at[which, group, space],
+            kv_buf.at[group, space, which],
             own_sem.at[which, group],
         )
 
@@ -139,47 +140,46 @@
 
     pl.semaphore_wait(barrier, chips + tm_count - 1)
 
-    def direct(which, group, step):
+    def direct(group, step):
         peer = lax.rem(chip + step, chips) * 2 + core
-        source = (k_ref, v_ref)[which]
-        return remote(
-            source.at[:, pl.ds(group * width, width)],
-            kv_buf.at[which, group, space],
-            kv_send.at[which, group, step],
-            kv_recv.at[which, group, step],
+        return remote(
+            kv_buf.at[group, space],
+            kv_buf.at[group, space],
+            kv_send.at[group, step],
+            kv_recv.at[group, step],
             "space",
             peer,
         )
 
-    def direct_in(which, group, step):
+    def direct_in(group, step):
         sender = lax.rem(chip - step + chips, chips) * 2 + core
         return remote(
-            kv_buf.at[which, group, sender],
-            kv_buf.at[which, group, sender],
-            kv_send.at[which, group, step],
-            kv_recv.at[which, group, step],
+            kv_buf.at[group, sender],
+            kv_buf.at[group, sender],
+            kv_send.at[group, step],
+            kv_recv.at[group, step],
             "space",
             partner,
         )
 
-    def to_partner(which, group, step):
+    def to_partner(group, step):
         slot = lax.rem(chip - step + chips, chips) * 2 + core
         return remote(
-            kv_buf.at[which, group, slot],
-            kv_buf.at[which, group, slot],
-            relay_send.at[which, group, step],
-            relay_recv.at[which, group, step],
+            kv_buf.at[group, slot],
+            kv_buf.at[group, slot],
+            relay_send.at[group, step],
+            relay_recv.at[group, step],
             "space",
             partner,
         )
 
-    def from_partner(which, group, step):
+    def from_partner(group, step):
         slot = lax.rem(chip - step + chips, chips) * 2 + 1 - core
         return remote(
-            kv_buf.at[which, group, slot],
-            kv_buf.at[which, group, slot],
-            relay_send.at[which, group, step],
-            relay_recv.at[which, group, step],
+            kv_buf.at[group, slot],
+            kv_buf.at[group, slot],
+            relay_send.at[group, step],
+            relay_recv.at[group, step],
             "space",
             partner,
         )
@@ -209,16 +209,15 @@
 
     for group in range(GROUPS):
         for which in range(2):
-
-            def send_chip(step, carry):
-                direct(which, group, step).start()
-                return carry
-
-            lax.fori_loop(1, chips, send_chip, 0)
+            own_copy(which, group).wait()
+
+        def send_chip(step, carry):
+            direct(group, step).start()
+            return carry
+
+        lax.fori_loop(1, chips, send_chip, 0)
     for group in range(GROUPS):
-        for which in range(2):
-            own_copy(which, group).wait()
-            to_partner(which, group, 0).start()
+        to_partner(group, 0).start()
 
     for which in range(2):
         target = which * half_count + tm // 2
@@ -328,17 +327,53 @@
             a_buf.at[group, place], x_buf.at[group, half_count + place], self_sem.at[group]
         )
 
+    def take_group(group, sums):
+        squares, b_in, c_out = sums
+
+        def take_frame(step, carry):
+            frame_in(group, step).wait_recv()
+            return carry
+
+        def take_earlier(step, carry):
+            earlier_in(group, step).wait_recv()
+            return carry
+
+        lax.fori_loop(1, half_count, take_frame, 0)
+        own_frame(group).wait()
+
+        @pl.when(half == 1)
+        def _():
+            lax.fori_loop(0, half_count, take_earlier, 0)
+
+        span = slice(group * width, (group + 1) * width)
+        part = x_buf[group].astype(F32).reshape(2 * size, width)
+        squares = squares + jnp.sum(part * part, axis=-1, keepdims=True)
+        gained = (part * pre_ref[:, span]).astype(BF16)
+        n_buf[group] = gained
+        across = (((1,), (1,)), ((), ()))
+        b_in = b_in + lax.dot_general(
+            gained, w_in_ref[:, span], across, preferred_element_type=F32
+        )
+        c_out = c_out + lax.dot_general(
+            gained[size:], w_out_ref[:, span], across, preferred_element_type=F32
+        )
+        return squares, b_in, c_out
+
+    state = w_in_ref.shape[0]
+    sums = (
+        jnp.zeros((2 * size, 1), F32),
+        jnp.zeros((2 * size, state), F32),
+        jnp.zeros((size, state), F32),
+    )
     for group in range(GROUPS):
 
         def relay(step, carry):
-            for which in range(2):
-                direct_in(which, group, step).wait_recv()
-                to_partner(which, group, step).start()
+            direct_in(group, step).wait_recv()
+            to_partner(group, step).start()
             return carry
 
         def relayed(step, carry):
-            for which in range(2):
-                from_partner(which, group, step).wait_recv()
+            from_partner(group, step).wait_recv()
             return carry
 
         lax.fori_loop(1, chips, relay, 0)
@@ -347,8 +382,8 @@
             lanes = slice(local * HEAD_DIM, (local + 1) * HEAD_DIM)
             head = group * heads_here + local
             query = q_ref[:, head * HEAD_DIM : (head + 1) * HEAD_DIM]
-            key = kv_buf[0, group, :, :, lanes].reshape(space_count * tokens, HEAD_DIM)
-            value = kv_buf[1, group, :, :, lanes].reshape(space_count * tokens, HEAD_DIM)
+            key = kv_buf[group, :, 0, :, lanes].reshape(space_count * tokens, HEAD_DIM)
+            value = kv_buf[group, :, 1, :, lanes].reshape(space_count * tokens, HEAD_DIM)
             scores = (
                 lax.dot_general(
                     query, key, (((1,), (1,)), ((), ())), preferred_element_type=F32
@@ -376,44 +411,19 @@
 
         lax.fori_loop(1, half_count, send_frame, 0)
         own_frame(group).start()
-
-    squares = jnp.zeros((2 * size, 1), F32)
-    for group in range(GROUPS):
-
-        def take_frame(step, carry):
-            frame_in(group, step).wait_recv()
-            return carry
-
-        def take_earlier(step, carry):
-            earlier_in(group, step).wait_recv()
-            return carry
-
-        lax.fori_loop(1, half_count, take_frame, 0)
-        own_frame(group).wait()
-
-        @pl.when(half == 1)
-        def _():
-            lax.fori_loop(0, half_count, take_earlier, 0)
-
-        part = x_buf[group].astype(F32).reshape(2 * size, width)
-        squares = squares + jnp.sum(part * part, axis=-1, keepdims=True)
+        if group >= LAG:
+            sums = take_group(group - LAG, sums)
+
+    for group in range(max(0, GROUPS - LAG), GROUPS):
+        sums = take_group(group, sums)
+    squares, b_in, c_out = sums
     scale = lax.rsqrt(squares / channels + 1e-05)
-    state = w_in_ref.shape[0]
-    b_in = jnp.zeros((2 * size, state), F32)
-    c_out = jnp.zeros((size, state), F32)
     across = (((1,), (1,)), ((), ()))
-    for group in range(GROUPS):
-        span = slice(group * width, (group + 1) * width)
-        part = x_buf[group].astype(F32).reshape(2 * size, width)
-        normed = (part * scale * pre_ref[:, span]).astype(BF16)
-        n_buf[group] = normed
-        b_in = b_in + lax.dot_general(
-            normed, w_in_ref[:, span], across, preferred_element_type=F32
-        )
-        c_out = c_out + lax.dot_general(
-            normed[size:], w_out_ref[:, span], across, preferred_element_type=F32
-        )
-    gram = lax.dot_general(c_out, b_in, across, precision=high, preferred_element_type=F32)
+    gram = lax.dot_general(
+        c_out * scale[size:], b_in * scale, across, precision=high, preferred_element_type=F32
+    )
+    gram = gram * jnp.transpose(jnp.broadcast_to(scale, (2 * size, size)))
+    scale_own = scale[size:]
     squares = jnp.zeros((size, 1), F32)
     for head in range(SHARED_HEADS):
         group, local = head // heads_here, head % heads_here
@@ -421,7 +431,7 @@
         values = n_buf[group, :, lanes]
         mixing = (gram * d_buf[head]).astype(BF16)
         mixed = jnp.dot(mixing, values, preferred_element_type=F32)
-        mixed = mixed + skips_ref[head] * values[size:].astype(F32)
+        mixed = mixed + skips_ref[head] * scale_own * values[size:].astype(F32)
         y_buf[:, head * HEAD_DIM : (head + 1) * HEAD_DIM] = mixed
         squares = squares + jnp.sum(mixed * mixed, axis=-1, keepdims=True)
     scale = lax.rsqrt(squares / channels + 1e-05)
@@ -461,13 +471,11 @@
     for group in range(GROUPS):
 
         def sent_chip(step, carry):
-            for which in range(2):
-                direct(which, group, step).wait_send()
+            direct(group, step).wait_send()
             return carry
 
         def sent_partner(step, carry):
-            for which in range(2):
-                to_partner(which, group, step).wait_send()
+            to_partner(group, step).wait_send()
             return carry
 
         def sent_frame(step, carry):
@@ -546,7 +554,7 @@
             dma((2,)),
             dma((2,)),
             dma((2,)),
-            pltpu.VMEM((2, GROUPS, space_count, tokens, width), BF16),
+            pltpu.VMEM((GROUPS, space_count, 2, tokens, width), BF16),
             pltpu.VMEM((GROUPS, half_count, rows, width), BF16),
             pltpu.VMEM((GROUPS, tm_count, rows, width), BF16),
             pltpu.VMEM((GROUPS, 2 * size, width), BF16),
@@ -554,10 +562,10 @@
             pltpu.VMEM((half_count, rows, channels), BF16),
             pltpu.VMEM((SHARED_HEADS, size, 2 * size), F32),
             dma((2, GROUPS)),
-            dma((2, GROUPS, chips)),
-            dma((2, GROUPS, chips)),
-            dma((2, GROUPS, chips)),
-            dma((2, GROUPS, chips)),
+            dma((GROUPS, chips)),
+            dma((GROUPS, chips)),
+            dma((GROUPS, chips)),
+            dma((GROUPS, chips)),
             dma((GROUPS, half_count)),
             dma((GROUPS, half_count)),
             dma((GROUPS, half_count)),

time: 49.6 us -> 48.5 us (0.978)
  Pallas kernels: 47.2 us -> 46.1 us
    pallas_call x1, Pallas kernels: 47.2 us -> 46.1 us  [body(): pl.pallas_call(functools.partial(kernel, (space_count, tm_count, block_li...]
where the time goes in v4:
time: 48.5 us; the launch traced here: 48 us
  Pallas kernels  46.1 us (95%)
  local copies, waits for them, and re-layouts  1.88 us (4%)
    pallas_call x1, Pallas kernels, body(): pl.pallas_call(functools.partial(kernel, (space_count, tm_count, block_li...  46.1 us
    unnamed x1, local copies, waits for them, and re-layouts  1.88 us

profile of v4, /device:TPU:0, one launch (start us, length us, event | category | flops | bytes accessed | tf_op | source)
XLA Modules:
  0.0 48.0 jit_solution(371734334871354317)
XLA Ops:
  0.0 46.1 %attend_and_mix.1 = bf16[4,32,2048]{2,1,0:T(8,128)(2,1)} custom-call(s32[4,3]{1,0:T(4,128)} %lists_hbm.1, f32[16]{0:T(128)} %rates_hbm.1, f32[16]{0:T(128)} %skips_hbm.1, bf16[128,2048]{1,0:T(8,128)(2,1)} %bitcast.9, bf16[128,2048]{1,0:T(8,128)(2,1)} %bitcast.10, bf16[128,2048]{1,0:T(8,128)(2,1)} %bitcast.11, f32[8,16,16]{2,1,0:T(8,128)} %steps_hbm.1, ...), custom_call_target="tpu_custom_call" | custom-call | tf_op jit(solution)/shard_map/attend_and_mix/pallas_call | solution.py:538
  46.1 1.9 %copy.13 = bf16[1,128,2048]{2,1,0:T(8,128)(2,1)} copy(bf16[1,128,2048]{2,1,0:T(8,128)(2,1)} %bitcast.8) | data formatting | bytes 1048576
